TPU v7x, 32 devices: a whole 2x2x4 slice. The times are simulated.
32 devices in a mesh: tile: 8 (over z, y), ka: 4 (over x, core).
Axes of the slice: x: 2, y: 2, z: 4, core: 2. Of those that a mesh axis runs over, the one named last changes fastest.
Arguments:
- integrals: bfloat16 [640, 48, 640], P('tile', 'ka'), may hold values from -0.03125 to 0.03125
- amplitudes: bfloat16 [48, 640, 8, 640], P('ka', 'tile'), may hold values from -24 to 24
- virt_energy: float32 [640], replicated, may hold values from 0.5 to 3
- pair_energy: float32 [8], replicated, may hold values from -6 to -1
Outputs:
- update: bfloat16 [8, 640, 640], P('ka', 'tile')
All inputs are finite; a program needn't handle non-finite values.
Results may differ from a plain program's by a relative error of at most 0.001.
Values may be sent and summed in bfloat16 or wider, within the bound.
No kernel may reach another device: no remote copies, remote signals or barrier semaphores. Data moves between devices by JAX's collectives and lax.ppermute only.
A program may use at most 128 MiB of HBM per device.

v0:
```python
import jax
import jax.numpy as jnp
from jax import lax
from jax.sharding import PartitionSpec as P


def per_device(integrals, amplitudes, virt_energy, pair_energy):
    particle_hole = lax.all_to_all(amplitudes, "tile", split_axis=3, concat_axis=1, tiled=True)
    pair_count = particle_hole.shape[2]
    col_count = particle_hole.shape[3]
    summed = jnp.einsum(
        "cka,kcjb->jab",
        lax.all_gather(integrals, "tile", axis=0, tiled=True),
        particle_hole,
        preferred_element_type=jnp.float32,
    )
    tile_pos = lax.axis_index("tile")
    ka_pos = lax.axis_index("ka")
    local_pairs = pair_count // lax.axis_size("ka")
    own_virt = lax.dynamic_slice_in_dim(virt_energy, tile_pos * col_count, col_count, 0)
    own_pairs = lax.dynamic_slice_in_dim(pair_energy, ka_pos * local_pairs, local_pairs, 0)
    regrouped = lax.all_to_all(summed, "tile", split_axis=1, concat_axis=2, tiled=True)
    reduced = lax.psum_scatter(regrouped, "ka", scatter_dimension=0, tiled=True)
    denominator = own_virt[None, :, None] + virt_energy[None, None, :] - own_pairs[:, None, None]
    return (reduced / denominator).astype(jnp.bfloat16)


def solution(mesh):
    in_specs = (P("tile", "ka", None), P("ka", "tile", None, None), P(), P())
    out_specs = P("ka", "tile", None)
    return jax.shard_map(
        per_device, mesh=mesh, in_specs=in_specs, out_specs=out_specs, check_vma=False
    )
```

profile of v0, /device:TPU:0, one launch (start us, length us, event | category | flops | bytes accessed | tf_op | source)
XLA Modules:
  0.0 652.1 jit_solution(2694304044166551413)
XLA Ops:
  6.5 20.2 %copy.11 = bf16[12,80,8,640]{1,2,0,3:T(8,128)(2,1)} copy(bf16[12,80,8,640]{3,2,1,0:T(8,128)(2,1)} %param.5) | data formatting | bytes 19660800 | tf_op args[1]
  26.7 7.3 %all-to-all-start = ((bf16[12,80,8,640]{1,2,0,3:T(8,128)(2,1)}), bf16[12,80,8,640]{1,2,0,3:T(8,128)(2,1)}, u32[]{:S(2)}, u32[]{:S(2)}) async-start(bf16[12,80,8,640]{1,2,0,3:T(8,128)(2,1)} %copy.11), calls=%async_computation | async-start | bytes 31457280 | tf_op jit(solution)/shard_map/all_to_all | solution.py:8
  34.0 0.0 all-gather.2.cloned.1.call-start
  34.1 0.7 all-gather.2.cloned.1.call-update
  34.8 0.0 reduce-scatter.2.cloned.1.call-start
  34.8 458.2 %all-to-all-done = bf16[12,80,8,640]{1,2,0,3:T(8,128)(2,1)} async-done(((bf16[12,80,8,640]{1,2,0,3:T(8,128)(2,1)}), bf16[12,80,8,640]{1,2,0,3:T(8,128)(2,1)}, u32[]{:S(2)}, u32[]{:S(2)}) %all-to-all-start) | async-done | bytes 9830432 | tf_op jit(solution)/shard_map/all_to_all | solution.py:8
  493.0 17.9 %copy.17 = bf16[12,80,8,8,80]{1,3,4,0,2:T(8,128)(2,1)} copy(bf16[12,80,8,8,80]{1,2,0,4,3:T(8,128)(2,1)} %bitcast) | data formatting | bytes 19660800 | tf_op jit(solution)/shard_map/all_to_all | solution.py:8
  510.8 23.0 %all_to_all.29 = bf16[12,640,8,80]{1,3,0,2:T(8,128)(2,1)} reshape(bf16[12,8,80,8,80]{2,1,4,0,3:T(8,128)(2,1)} %bitcast.24) | data formatting | bytes 19660800 | tf_op jit(solution)/shard_map/all_to_all | solution.py:8
  533.9 0.0 all-gather.2.cloned.1.call-done
  533.9 13.0 %fusion.2 = f32[8,640,80]{1,2,0:T(8,128)} fusion(bf16[12,640,8,80]{1,3,0,2:T(8,128)(2,1)} %all_to_all.29, bf16[640,12,640]{2,0,1:T(8,128)(2,1)} %all-gather.2.cloned.1.call-done), kind=kOutput, calls=%fused_computation.3 | convolution fusion | flops 6291456000 | bytes 21299200 | tf_op jit(solution)/shard_map/cka,kcjb->jab/dot_general | solution.py:11
  546.9 0.0 copy-start.1
  546.9 0.0 copy-start
  546.9 2.4 copy.13
  549.3 63.0 %all_to_all.36 = f32[8,640,80]{2,0,1:T(8,128)S(1)} all-to-all(f32[8,640,80]{2,0,1:T(8,128)S(1)} %copy.13), channel_id=1, replica_groups=mesh['tile'=8,'ka'=4] {'tile'}, dimensions={1} | all-to-all | bytes 3276800 | tf_op jit(solution)/shard_map/all_to_all | solution.py:22
  612.4 1.5 copy.14
  613.9 1.7 all_to_all.33
  615.6 0.0 reduce-scatter.2.cloned.1.call-update
  615.7 0.0 copy-done.1
  615.7 0.1 dynamic_slice.7
  615.8 0.0 copy-done
  615.8 0.1 dynamic_slice.6
  615.8 0.1 broadcast_add_fusion
  615.9 27.5 %reduce-scatter.2.cloned.1.call-done = f32[2,80,640]{2,1,0:T(8,128)} async-done(((f32[8,80,640]{2,1,0:T(8,128)}), f32[2,80,640]{2,1,0:T(8,128)}) %reduce-scatter.2.cloned.1.call-update) | async-done | bytes 409616 | tf_op jit(solution)/shard_map/reduce_scatter | solution.py:23
  643.5 1.8 divide_convert_fusion
Async XLA Ops:
  26.7 466.2 %all-to-all-start = ((bf16[12,80,8,640]{1,2,0,3:T(8,128)(2,1)}), bf16[12,80,8,640]{1,2,0,3:T(8,128)(2,1)}, u32[]{:S(2)}, u32[]{:S(2)}) async-start(bf16[12,80,8,640]{1,2,0,3:T(8,128)(2,1)} %copy.11), calls=%async_computation | async-start | bytes 31457280 | tf_op jit(solution)/shard_map/all_to_all | solution.py:8
  34.0 499.9 %all-gather.2.cloned.1.call-start = ((), (), s32[]{:S(2)}) async-start(), calls=%async_computation.3 | async-start | bytes 11059200 | tf_op jit(solution)/shard_map/all_gather | solution.py:13
  34.8 608.7 %reduce-scatter.2.cloned.1.call-start = ((), (), s32[]{:S(2)}) async-start(), calls=%async_computation.4 | async-start | bytes 2048000 | tf_op jit(solution)/shard_map/reduce_scatter | solution.py:23
  546.9 68.8 %copy-start.1 = (f32[8]{0:T(128)S(1)}, f32[8]{0:T(128)}, u32[]{:S(2)}) copy-start(f32[8]{0:T(128)} %param.7) | copy-start | bytes 100
  546.9 68.9 %copy-start = (f32[640]{0:T(1024)S(1)}, f32[640]{0:T(1024)}, u32[]{:S(2)}) copy-start(f32[640]{0:T(1024)} %param.6) | copy-start | bytes 7684
Sparse Core Ops, SparseCore 0:
  37.1 412.8 all-gather.1
  615.8 27.6 reduce-scatter.1
where the time goes:
time: 654 us; the launch traced here: 652 us
  waiting for transfers between devices  486 us (74%)
  local copies, waits for them, and re-layouts  67 us (10%)
  blocking collectives  63 us (10%)
  between operations  13.4 us (2%)
  matrix products  13 us (2%)
  starting transfers between devices  7.36 us (1%)
    all_to_all x1, waiting for transfers between devices, per_device(): lax.all_to_all(amplitudes, 'tile', split_axis=3, concat_axis=1, tiled=True)  458 us
    all_to_all x1, blocking collectives, per_device(): lax.all_to_all(summed, 'tile', split_axis=1, concat_axis=2, tiled=True)  63 us
    all_to_all x2, local copies, waits for them, and re-layouts, per_device(): lax.all_to_all(amplitudes, 'tile', split_axis=3, concat_axis=1, tiled=True)  40.9 us
    reduce_scatter x1, waiting for transfers between devices, per_device(): reduced = lax.psum_scatter(regrouped, 'ka', scatter_dimension=0, tiled=True)  27.5 us
    unnamed x5, local copies, waits for them, and re-layouts  20.2 us
  transfers between devices with their start and end apart: 3, of which 2 were waited for; matrix products, arithmetic and copies ran while one was open for 3% of the time, Pallas kernels for 0%

commit v1 on v0

--- a/solution.py
+++ b/solution.py
@@ -2,6 +2,18 @@
 import jax.numpy as jnp
 from jax import lax
 from jax.sharding import PartitionSpec as P
+
+
+def cut_along(shard, dim, peers):
+    dims = shard.shape
+    tiles = shard.reshape(*dims[:dim], peers, dims[dim] // peers, *dims[dim + 1 :])
+    return jnp.moveaxis(tiles, dim, 0)
+
+
+def laid_out(parts, dim):
+    parts = jnp.moveaxis(parts, 0, dim)
+    shape = parts.shape
+    return parts.reshape(*shape[:dim], shape[dim] * shape[dim + 1], *shape[dim + 2 :])
 
 
 def per_device(integrals, amplitudes, virt_energy, pair_energy):
@@ -19,7 +31,14 @@
     local_pairs = pair_count // lax.axis_size("ka")
     own_virt = lax.dynamic_slice_in_dim(virt_energy, tile_pos * col_count, col_count, 0)
     own_pairs = lax.dynamic_slice_in_dim(pair_energy, ka_pos * local_pairs, local_pairs, 0)
-    regrouped = lax.all_to_all(summed, "tile", split_axis=1, concat_axis=2, tiled=True)
+    size, position = (lax.axis_size("tile"), lax.axis_index("tile"))
+    parts = cut_along(summed, 1, size)
+    finished = [parts[position]]
+    for turn in range(1, size):
+        sent = parts[position ^ turn]
+        finished.append(lax.ppermute(sent, "tile", [(i, i ^ turn) for i in range(size)]))
+    parts = jnp.stack(finished)[position ^ jnp.arange(size)]
+    regrouped = laid_out(parts, 2)
     reduced = lax.psum_scatter(regrouped, "ka", scatter_dimension=0, tiled=True)
     denominator = own_virt[None, :, None] + virt_energy[None, None, :] - own_pairs[:, None, None]
     return (reduced / denominator).astype(jnp.bfloat16)

time: 654 us -> 668 us (1.021)
  blocking collectives: 63 us -> 0 us
  waiting for transfers between devices: 486 us -> 530 us
  local copies, waits for them, and re-layouts: 67 us -> 90.7 us
  starting transfers between devices: 7.36 us -> 16.3 us
    all_to_all x1 -> x0, blocking collectives: 63 us -> none  [per_device(): lax.all_to_all(summed, 'tile', split_axis=1, concat_axis=2, tiled=True)]
    ppermute x0 -> x7, waiting for transfers between devices: none -> 35.1 us  [per_device(): lax.ppermute(sent, 'tile', [(i, i ^ turn) for i in range(size)])]
    another operation x0 -> x10, local copies, waits for them, and re-layouts: none -> 10.5 us
    reduce_scatter x1, waiting for transfers between devices: 27.5 us -> 36.5 us  [per_device(): reduced = lax.psum_scatter(regrouped, 'ka', scatter_dimension=0, tiled=True)]
    ppermute x0 -> x7, starting transfers between devices: none -> 8.97 us  [per_device(): lax.ppermute(sent, 'tile', [(i, i ^ turn) for i in range(size)])]
    unnamed x5 -> x16, local copies, waits for them, and re-layouts: 20.2 us -> 28.3 us
  transfers between devices with their start and end apart: 3 -> 10, of which waited for: 2 -> 5; matrix products, arithmetic and copies ran while one was open for 3% -> 4% of each run, Pallas kernels for 0% -> 0%
where the time goes in v1:
time: 668 us; the launch traced here: 666 us
  waiting for transfers between devices  530 us (79%)
  local copies, waits for them, and re-layouts  90.7 us (14%)
  starting transfers between devices  16.3 us (2%)
  between operations  13.6 us (2%)
  matrix products  13 us (2%)
    all_to_all x1, waiting for transfers between devices, per_device(): lax.all_to_all(amplitudes, 'tile', split_axis=3, concat_axis=1, tiled=True)  458 us
    all_to_all x2, local copies, waits for them, and re-layouts, per_device(): lax.all_to_all(amplitudes, 'tile', split_axis=3, concat_axis=1, tiled=True)  40.9 us
    reduce_scatter x1, waiting for transfers between devices, per_device(): reduced = lax.psum_scatter(regrouped, 'ka', scatter_dimension=0, tiled=True)  36.5 us
    ppermute x7, waiting for transfers between devices, per_device(): lax.ppermute(sent, 'tile', [(i, i ^ turn) for i in range(size)])  35.1 us
    unnamed x16, local copies, waits for them, and re-layouts  28.3 us
  transfers between devices with their start and end apart: 10, of which 5 were waited for; matrix products, arithmetic and copies ran while one was open for 4% of the time, Pallas kernels for 0%

profile of v1, /device:TPU:0, one launch (start us, length us, event | category | flops | bytes accessed | tf_op | source)
XLA Modules:
  0.0 665.9 jit_solution(3112469908212230939)
XLA Ops:
  6.5 20.2 %copy.36 = bf16[12,80,8,640]{1,2,0,3:T(8,128)(2,1)} copy(bf16[12,80,8,640]{3,2,1,0:T(8,128)(2,1)} %param.5) | data formatting | bytes 19660800 | tf_op args[1]
  26.7 7.3 %all-to-all-start = ((bf16[12,80,8,640]{1,2,0,3:T(8,128)(2,1)}), bf16[12,80,8,640]{1,2,0,3:T(8,128)(2,1)}, u32[]{:S(2)}, u32[]{:S(2)}) async-start(bf16[12,80,8,640]{1,2,0,3:T(8,128)(2,1)} %copy.36), calls=%async_computation | async-start | bytes 31457280 | tf_op jit(solution)/shard_map/all_to_all | solution.py:20
  34.0 0.0 all-gather.2.cloned.1.call-start
  34.0 0.7 all-gather.2.cloned.1.call-update
  34.7 0.0 reduce-scatter.2.cloned.1.call-start
  34.8 458.1 %all-to-all-done = bf16[12,80,8,640]{1,2,0,3:T(8,128)(2,1)} async-done(((bf16[12,80,8,640]{1,2,0,3:T(8,128)(2,1)}), bf16[12,80,8,640]{1,2,0,3:T(8,128)(2,1)}, u32[]{:S(2)}, u32[]{:S(2)}) %all-to-all-start) | async-done | bytes 9830432 | tf_op jit(solution)/shard_map/all_to_all | solution.py:20
  492.9 17.9 %copy.49 = bf16[12,80,8,8,80]{1,3,4,0,2:T(8,128)(2,1)} copy(bf16[12,80,8,8,80]{1,2,0,4,3:T(8,128)(2,1)} %bitcast) | data formatting | bytes 19660800 | tf_op jit(solution)/shard_map/all_to_all | solution.py:20
  510.8 23.1 %all_to_all.16 = bf16[12,640,8,80]{1,3,0,2:T(8,128)(2,1)} reshape(bf16[12,8,80,8,80]{2,1,4,0,3:T(8,128)(2,1)} %bitcast.49) | data formatting | bytes 19660800 | tf_op jit(solution)/shard_map/all_to_all | solution.py:20
  533.9 0.0 all-gather.2.cloned.1.call-done
  533.9 13.0 %fusion.2 = f32[8,640,80]{1,2,0:T(8,128)} fusion(bf16[12,640,8,80]{1,3,0,2:T(8,128)(2,1)} %all_to_all.16, bf16[640,12,640]{2,0,1:T(8,128)(2,1)} %all-gather.2.cloned.1.call-done), kind=kOutput, calls=%fused_computation.4 | convolution fusion | flops 6291456000 | bytes 21299200 | tf_op jit(solution)/shard_map/cka,kcjb->jab/dot_general | solution.py:23
  546.9 2.4 reshape.70
  549.2 3.2 constant_dynamic-slice_fusion
  552.4 0.0 copy-start.1
  552.4 0.0 copy-start
  552.4 1.2 copy.38
  553.6 1.9 copy.39
  555.5 1.4 collective-permute-start
  556.9 1.8 copy.40
  558.7 0.0 collective-permute-start.1
  558.8 1.1 copy.41
  559.9 2.1 collective-permute-start.2
  562.0 0.0 copy-done.1
  562.0 0.1 copy.42
  562.1 0.1 collective-permute-start.3
  562.2 0.0 copy-done
  562.2 0.1 copy.43
  562.4 3.8 collective-permute-start.4
  566.2 0.1 copy.44
  566.4 0.1 copy.45
  566.5 0.7 bitcast_dynamic-update-slice_fusion.7
  567.3 0.0 collective-permute-done
  567.3 1.5 collective-permute-start.5
  568.7 1.7 bitcast_dynamic-update-slice_fusion.6
  570.5 10.5 %collective-permute-done.1 = f32[8,80,80]{2,1,0:T(8,128)} collective-permute-done((f32[8,80,80]{2,1,0:T(8,128)}, f32[8,80,80]{2,1,0:T(8,128)}, u32[]{:S(2)}, u32[]{:S(2)}) %collective-permute-start.1) | collective-permute-done | bytes 204832 | tf_op jit(solution)/shard_map/ppermute | solution.py:39
  581.0 0.0 collective-permute-start.6
  581.0 1.7 bitcast_dynamic-update-slice_fusion.5
  582.7 1.6 collective-permute-done.2
  584.3 1.7 bitcast_dynamic-update-slice_fusion.4
  586.0 0.0 collective-permute-done.3
  586.0 0.7 bitcast_dynamic-update-slice_fusion.3
  586.7 23.0 %collective-permute-done.4 = f32[8,80,80]{2,1,0:T(8,128)S(1)} collective-permute-done((f32[8,80,80]{2,1,0:T(8,128)S(1)}, f32[8,80,80]{2,1,0:T(8,128)S(1)}, u32[]{:S(2)}, u32[]{:S(2)}) %collective-permute-start.4) | collective-permute-done | bytes 204832 | tf_op jit(solution)/shard_map/ppermute | solution.py:39
  609.7 0.7 bitcast_dynamic-update-slice_fusion.2
  610.5 0.0 collective-permute-done.5
  610.5 0.7 bitcast_dynamic-update-slice_fusion.1
  611.2 0.0 collective-permute-done.6
  611.2 0.8 bitcast_dynamic-update-slice_fusion
  612.0 2.5 gather_fusion
  614.4 3.0 copy.46
  617.5 0.0 copy-start.3
  617.5 0.0 copy-start.2
  617.5 3.0 reshape.71
  620.5 0.0 reduce-scatter.2.cloned.1.call-update
  620.5 0.0 copy-done.3
  620.5 0.1 dynamic_slice.8
  620.6 0.0 copy-done.2
  620.6 0.1 dynamic_slice.7
  620.7 0.1 broadcast_add_fusion
  620.8 36.5 %reduce-scatter.2.cloned.1.call-done = f32[2,80,640]{2,1,0:T(8,128)} async-done(((f32[8,80,640]{2,1,0:T(8,128)}), f32[2,80,640]{2,1,0:T(8,128)}) %reduce-scatter.2.cloned.1.call-update) | async-done | bytes 409616 | tf_op jit(solution)/shard_map/reduce_scatter | solution.py:42
  657.3 1.8 divide_convert_fusion
  (2 shorter events, 0.0 us)
Async XLA Ops:
  26.7 466.2 %all-to-all-start = ((bf16[12,80,8,640]{1,2,0,3:T(8,128)(2,1)}), bf16[12,80,8,640]{1,2,0,3:T(8,128)(2,1)}, u32[]{:S(2)}, u32[]{:S(2)}) async-start(bf16[12,80,8,640]{1,2,0,3:T(8,128)(2,1)} %copy.36), calls=%async_computation | async-start | bytes 31457280 | tf_op jit(solution)/shard_map/all_to_all | solution.py:20
  34.0 499.9 %all-gather.2.cloned.1.call-start = ((), (), s32[]{:S(2)}) async-start(), calls=%async_computation.2 | async-start | bytes 11059200 | tf_op jit(solution)/shard_map/all_gather | solution.py:25
  34.7 622.6 %reduce-scatter.2.cloned.1.call-start = ((), (), s32[]{:S(2)}) async-start(), calls=%async_computation.3 | async-start | bytes 2048000 | tf_op jit(solution)/shard_map/reduce_scatter | solution.py:42
  552.4 9.6 %copy-start.1 = (f32[8,1,80,80]{2,1,3,0:T(1,128)S(1)}, f32[8,1,80,80]{2,1,3,0:T(1,128)}, u32[]{:S(2)}) copy-start(f32[8,1,80,80]{2,1,3,0:T(1,128)} %get-tuple-element.8) | copy-start | bytes 614404
  552.4 9.8 %copy-start = (f32[8,1,80,80]{2,1,3,0:T(1,128)S(1)}, f32[8,1,80,80]{2,1,3,0:T(1,128)}, u32[]{:S(2)}) copy-start(f32[8,1,80,80]{2,1,3,0:T(1,128)} %get-tuple-element.7) | copy-start | bytes 614404
  555.5 11.8 %collective-permute-start = (f32[8,80,80]{2,1,0:T(8,128)}, f32[8,80,80]{2,1,0:T(8,128)}, u32[]{:S(2)}, u32[]{:S(2)}) collective-permute-start(f32[8,80,80]{2,1,0:T(8,128)} %bitcast.7), channel_id=1, source_target_pairs={{0,4},{4,0},{8,12},{12,8},{16,20},{20,16},{24,28},{28,24},{1,5},{5... | collective-permute-start | bytes 614408 | tf_op jit(solution)/shard_map/ppermute | solution.py:39
  558.7 22.2 %collective-permute-start.1 = (f32[8,80,80]{2,1,0:T(8,128)}, f32[8,80,80]{2,1,0:T(8,128)}, u32[]{:S(2)}, u32[]{:S(2)}) collective-permute-start(f32[8,80,80]{2,1,0:T(8,128)} %bitcast.9), channel_id=1, source_target_pairs={{0,8},{4,12},{8,0},{12,4},{16,24},{20,28},{24,16},{28,20},{1,9},{5... | collective-permute-start | bytes 614408 | tf_op jit(solution)/shard_map/ppermute | solution.py:39
  559.9 24.4 %collective-permute-start.2 = (f32[8,80,80]{2,1,0:T(8,128)S(1)}, f32[8,80,80]{2,1,0:T(8,128)}, u32[]{:S(2)}, u32[]{:S(2)}) collective-permute-start(f32[8,80,80]{2,1,0:T(8,128)S(1)} %bitcast.55), channel_id=1, source_target_pairs={{0,12},{4,8},{8,4},{12,0},{16,28},{20,24},{24,20},{28,16},{1,13},{... | collective-permute-start | bytes 614408 | tf_op jit(solution)/shard_map/ppermute | solution.py:39
  562.1 23.9 %collective-permute-start.3 = (f32[8,80,80]{2,1,0:T(8,128)S(1)}, f32[8,80,80]{2,1,0:T(8,128)S(1)}, u32[]{:S(2)}, u32[]{:S(2)}) collective-permute-start(f32[8,80,80]{2,1,0:T(8,128)S(1)} %bitcast.54), channel_id=1, source_target_pairs={{0,16},{4,20},{8,24},{12,28},{16,0},{20,4},{24,8},{28,12},{1,17},{... | collective-permute-start | bytes 614408 | tf_op jit(solution)/shard_map/ppermute | solution.py:39
  562.4 47.4 %collective-permute-start.4 = (f32[8,80,80]{2,1,0:T(8,128)S(1)}, f32[8,80,80]{2,1,0:T(8,128)S(1)}, u32[]{:S(2)}, u32[]{:S(2)}) collective-permute-start(f32[8,80,80]{2,1,0:T(8,128)S(1)} %bitcast.53), channel_id=1, source_target_pairs={{0,20},{4,16},{8,28},{12,24},{16,4},{20,0},{24,12},{28,8},{1,21},{... | collective-permute-start | bytes 614408 | tf_op jit(solution)/shard_map/ppermute | solution.py:39
  567.3 43.2 %collective-permute-start.5 = (f32[8,80,80]{2,1,0:T(8,128)S(1)}, f32[8,80,80]{2,1,0:T(8,128)S(1)}, u32[]{:S(2)}, u32[]{:S(2)}) collective-permute-start(f32[8,80,80]{2,1,0:T(8,128)S(1)} %bitcast.52), channel_id=1, source_target_pairs={{0,24},{4,28},{8,16},{12,20},{16,8},{20,12},{24,0},{28,4},{1,25},{... | collective-permute-start | bytes 614408 | tf_op jit(solution)/shard_map/ppermute | solution.py:39
  581.0 30.3 %collective-permute-start.6 = (f32[8,80,80]{2,1,0:T(8,128)S(1)}, f32[8,80,80]{2,1,0:T(8,128)S(1)}, u32[]{:S(2)}, u32[]{:S(2)}) collective-permute-start(f32[8,80,80]{2,1,0:T(8,128)S(1)} %bitcast.51), channel_id=1, source_target_pairs={{0,28},{4,24},{8,20},{12,16},{16,12},{20,8},{24,4},{28,0},{1,29},{... | collective-permute-start | bytes 614408 | tf_op jit(solution)/shard_map/ppermute | solution.py:39
  617.5 3.1 copy-start.3
  617.5 3.2 copy-start.2
Sparse Core Ops, SparseCore 0:
  37.1 412.8 all-gather.1
  620.6 36.5 reduce-scatter.1
